TPU v7x, 32 devices: a whole 2x2x4 slice. The times are simulated.
32 devices in a mesh: inner: 8 (over z, y), cols: 4 (over x, core).
Axes of the slice: x: 2, y: 2, z: 4, core: 2. Of those that a mesh axis runs over, the one named last changes fastest.
Arguments:
- left_u: bfloat16 [64, 512, 128], P(('inner', 'cols')), may hold values from -6 to 6
- left_v: bfloat16 [64, 512, 128], P(('inner', 'cols')), may hold values from -0.0234375 to 0.0234375
- right_u: bfloat16 [16, 64, 512, 128], P('cols', 'inner'), may hold values from -6 to 6
- right_v: bfloat16 [16, 64, 512, 128], P('cols', 'inner'), may hold values from -0.1875 to 0.1875
- sketch: bfloat16 [16, 512, 128], P('cols'), may hold values from -0.25 to 0.25
- tile_index: int32 [16, 64], P('cols', 'inner'), may hold values from 0 to 63, as said below
- slot_mask: int32 [16, 64], P('cols', 'inner'), may hold values from 0 to 1, as said below
Outputs:
- basis: float32 [16, 512, 128], P('cols', 'inner')
- coeff: float32 [16, 512, 128], P('cols', 'inner')
Inputs may be any that keep to these rules, and one draw needn't show every extreme that they name: `tile_index`: slot s of an output tile belongs to inner group g = s // 8 and names a left tile of that group, g * 8 to g * 8 + 7; the tiles named by one output tile's slots of one group are distinct. `slot_mask`: in each output tile and inner group the live slots come first and there is at least one; in every output tile some group has all 8 slots live, and the others at most 4.
All inputs are finite; a program needn't handle non-finite values.
Results may differ from a plain program's by a relative error of at most 0.0045.
Values may be sent and summed in bfloat16 or wider, within the bound.
A program may use at most 64 MiB of HBM per device.

v0:
```python
import math
import jax
import jax.numpy as jnp
from jax import lax
from jax.sharding import PartitionSpec as P

NB = 512
HIGH = lax.Precision.HIGHEST


def orthonormal(sketch_rows, factor):
    solved = jax.scipy.linalg.solve_triangular(factor, jnp.swapaxes(sketch_rows, 1, 2), lower=True)
    return jnp.swapaxes(solved, 1, 2)


def gram_of(sketch_rows):
    return jnp.einsum("ona,onb->oab", sketch_rows, sketch_rows, precision=HIGH)


def body(left_u, left_v, right_u, right_v, sketch, tile_index, slot_mask):
    group_u, group_v = (
        lax.all_gather(left_u, "cols", axis=0, tiled=True),
        lax.all_gather(left_v, "cols", axis=0, tiled=True),
    )
    group_tiles = group_u.shape[0]
    local_idx = tile_index - lax.axis_index("inner") * group_tiles
    live_mask = slot_mask.astype(jnp.float32)[..., None, None]
    tile_u = jnp.take(group_u, local_idx, axis=0)
    tile_v = jnp.take(group_v, local_idx, axis=0)
    pairing = jnp.einsum("osna,osnb->osab", tile_v, right_u, preferred_element_type=jnp.float32)
    probes = jnp.einsum("osnb,ont->osbt", right_v, sketch, preferred_element_type=jnp.float32)
    mixing = (live_mask * jnp.einsum("osab,osbt->osat", pairing, probes, precision=HIGH)).astype(
        jnp.bfloat16
    )
    partial_sketch = jnp.einsum(
        "osna,osat->ont", tile_u, mixing, preferred_element_type=jnp.float32
    )
    scale_up = math.sqrt(NB)
    summed = lax.psum(partial_sketch, "inner")
    factor = jnp.linalg.cholesky(gram_of(summed))
    ortho = orthonormal(summed, factor)
    row_count = summed.shape[1] // lax.axis_size("inner")
    row_start = lax.axis_index("inner") * row_count
    basis = lax.dynamic_slice_in_dim(ortho, row_start, row_count, 1) * scale_up
    full_basis = ortho.astype(jnp.bfloat16)
    projected = jnp.einsum("osna,ont->osat", tile_u, full_basis, preferred_element_type=jnp.float32)
    backward = (
        live_mask * jnp.einsum("osab,osat->osbt", pairing, projected, precision=HIGH)
    ).astype(jnp.bfloat16)
    coeff_terms = jnp.einsum(
        "osnb,osbt->ont", right_v, backward, preferred_element_type=jnp.float32
    )
    coeff = lax.psum_scatter(coeff_terms, "inner", scatter_dimension=1, tiled=True)
    return (basis, coeff)


def solution(mesh):
    return jax.shard_map(
        body,
        mesh=mesh,
        in_specs=(
            P(("inner", "cols"), None, None),
            P(("inner", "cols"), None, None),
            P("cols", "inner", None, None),
            P("cols", "inner", None, None),
            P("cols", None, None),
            P("cols", "inner"),
            P("cols", "inner"),
        ),
        out_specs=(P("cols", "inner", None), P("cols", "inner", None)),
        check_vma=False,
    )
```

profile of v0, /device:TPU:0, one launch (start us, length us, event | category | flops | bytes accessed | tf_op | source)
XLA Modules:
  0.0 335.3 jit_solution(5929237776262730713)
XLA Ops:
  7.2 0.0 copy-start
  7.2 0.0 all-gather.5.cloned.1.call-start
  7.2 0.7 all-gather.5.cloned.1.call-update
  7.9 0.0 all-gather.3.cloned.1.call-start
  8.0 0.7 all-gather.3.cloned.1.call-update
  8.7 0.0 all-reduce.4.cloned.1.call-start
  8.7 0.7 compare_and_fusion
  9.4 0.1 reshape.41
  9.5 0.7 convert_element_type.12
  10.2 0.0 copy-done
  10.2 3.8 %fusion.10 = f32[4,8,128,128]{3,2,1,0:T(8,128)S(1)} fusion(bf16[4,8,512,128]{3,2,1,0:T(8,128)(2,1)} %param.12, bf16[4,512,128]{2,1,0:T(8,128)(2,1)S(1)} %copy-done), kind=kOutput, calls=%fused_computation.16 | convolution fusion | flops 536870912 | bytes 6815744 | tf_op jit(solution)/shard_map/osnb,ont->osbt/dot_general | solution.py:31
  14.0 15.0 %all-gather.5.cloned.1.call-done = bf16[8,512,128]{2,1,0:T(8,128)(2,1)} async-done(((bf16[2,512,128]{2,1,0:T(8,128)(2,1)}), bf16[8,512,128]{2,1,0:T(8,128)(2,1)}) %all-gather.5.cloned.1.call-update) | async-done | bytes 1048592 | tf_op jit(solution)/shard_map/all_gather | solution.py:23
  29.0 4.3 %gather_fusion.1 = bf16[32,512,128]{2,1,0:T(8,128)(2,1)} fusion(bf16[8,512,128]{2,1,0:T(8,128)(2,1)} %all-gather.5.cloned.1.call-done, s32[1024]{0:T(1024)S(1)} %pad_clamp_fusion), kind=kCustom, calls=%fused_computation.1.clone | custom fusion | bytes 8388736 | tf_op jit(solution)/shard_map/jit(_take)/gather | solution.py:29
  33.3 6.3 %copy.23 = bf16[4,8,512,128]{2,3,1,0:T(8,128)(2,1)} copy(bf16[4,8,512,128]{3,2,1,0:T(8,128)(2,1)} %bitcast.43) | data formatting | bytes 8388608 | tf_op jit(solution)/shard_map/jit(_take)/gather | solution.py:29
  39.6 7.7 %all-gather.3.cloned.1.call-done = bf16[8,512,128]{2,1,0:T(8,128)(2,1)} async-done(((bf16[2,512,128]{2,1,0:T(8,128)(2,1)}), bf16[8,512,128]{2,1,0:T(8,128)(2,1)}) %all-gather.3.cloned.1.call-update) | async-done | bytes 1048592 | tf_op jit(solution)/shard_map/all_gather | solution.py:22
  47.3 4.3 %gather_fusion = bf16[32,512,128]{2,1,0:T(8,128)(2,1)} fusion(bf16[8,512,128]{2,1,0:T(8,128)(2,1)} %all-gather.3.cloned.1.call-done, s32[1024]{0:T(1024)S(1)} %pad_clamp_fusion), kind=kCustom, calls=%fused_computation.clone | custom fusion | bytes 8388736 | tf_op jit(solution)/shard_map/jit(_take)/gather | solution.py:28
  51.6 6.2 %copy.22 = bf16[4,8,512,128]{2,3,1,0:T(8,128)(2,1)} copy(bf16[4,8,512,128]{3,2,1,0:T(8,128)(2,1)} %bitcast.42) | data formatting | bytes 8388608 | tf_op jit(solution)/shard_map/jit(_take)/gather | solution.py:28
  57.7 4.8 %fusion = f32[4,8,128,128]{3,2,1,0:T(8,128)S(1)} fusion(bf16[4,8,512,128]{3,2,1,0:T(8,128)(2,1)} %param.11, bf16[4,8,512,128]{2,3,1,0:T(8,128)(2,1)} %copy.23, pred[4,8]{1,0:T(4,128)(4,1)S(1)} %get-tuple-element.9), kind=kOutput, calls=%fused_computation.2 | convolution fusion | flops 538968064 | bytes 10485792 | tf_op jit(solution)/shard_map/osna,osnb->osab/dot_general | solution.py:30
  62.5 0.0 copy-start.3
  62.6 1.3 copy-done.3
  63.9 0.0 copy-start.5
  63.9 2.3 multiply_convert_fusion.1
  66.2 0.0 copy-done.5
  66.2 2.8 fusion.8
  69.0 0.0 all-reduce.4.cloned.1.call-update
  69.0 0.2 all-reduce.6.cloned.1.call-start
  69.3 78.1 %all-reduce.4.cloned.1.call-done = f32[4,512,128]{2,1,0:T(8,128)} async-done(((f32[4,512,128]{2,1,0:T(8,128)}), f32[4,512,128]{2,1,0:T(8,128)}) %all-reduce.4.cloned.1.call-update) | async-done | bytes 1048592 | tf_op jit(solution)/shard_map/psum | solution.py:39
  147.4 0.0 copy-start.2
  147.4 3.4 %fusion.19 = f32[4,128,128]{2,1,0:T(8,128)S(1)} fusion(f32[4,512,128]{2,1,0:T(8,128)} %all-reduce.4.cloned.1.call-done), kind=kOutput, calls=%fused_computation.36 | convolution fusion | flops 402653184 | bytes 1310720 | tf_op jit(solution)/shard_map/ona,onb->oab/dot_general | solution.py:17
  150.8 0.1 copy.27
  151.0 46.9 %custom-call.8 = f32[4,128,128]{2,1,0:T(8,128)S(1)} custom-call(f32[4,128,128]{2,1,0:T(8,128)S(1)} %fusion.15), custom_call_target="Cholesky" | custom-call | tf_op jit(solution)/shard_map/jit(cholesky)/cholesky | solution.py:40
  198.0 0.1 compare_reduce_fusion
  198.1 0.1 select_bitcast_fusion
  198.2 39.5 %custom-call.9 = f32[4,1,128,128]{2,3,1,0:T(8,128)S(1)} custom-call(f32[4,1,128,128]{3,2,1,0:T(8,128)S(1)} %select_bitcast_fusion), custom_call_target="InvertDiagBlocksLowerTriangular" | custom-call | tf_op jit(solution)/shard_map/jit(_solve_triangular)/vmap()/triangular_solve | solution.py:12
  237.7 0.0 copy-done.2
  237.7 1.0 fusion.13
  238.8 0.0 copy-start.4
  238.8 3.6 %fusion.3 = f32[4,8,128,128]{3,2,1,0:T(8,128)S(1)} fusion(bf16[4,8,512,128]{2,3,1,0:T(8,128)(2,1)} %copy.22, pred[4,8]{1,0:T(4,128)(4,1)S(1)} %get-tuple-element.9, f32[4,512,128]{2,1,0:T(8,128)S(1)} %fusion.13), kind=kOutput, calls=%fused_computation.6 | convolution fusion | flops 539230208 | bytes 7340064 | tf_op jit(solution)/shard_map/osna,ont->osat/dot_general | solution.py:46
  242.4 0.0 copy-done.4
  242.4 0.0 copy-start.1
  242.5 3.7 %multiply_convert_fusion = bf16[4,8,128,128]{3,2,1,0:T(8,128)(2,1)S(1)} fusion(f32[4,8,128,128]{3,2,1,0:T(8,128)S(1)} %copy-done.4, f32[4,8,128,128]{3,2,1,0:T(8,128)S(1)} %fusion.3, f32[4,8]{1,0:T(4,128)S(1)} %convert_element_type.12), kind=kOutput, calls=%fused_computation.11 | convolution fusion | flops 806354944 | bytes 5243008 | tf_op jit(solution)/shard_map/osab,osat->osbt/dot_general | solution.py:48
  246.2 0.0 copy-done.1
  246.2 0.0 copy-start.6
  246.2 1.5 convolution_bitcast_fusion
  247.7 1.4 copy.31
  249.1 0.0 all-reduce.6.cloned.1.call-update
  249.1 0.0 copy-done.6
  249.2 0.6 dynamic-slice
  250.4 0.7 dynamic-slice_multiply_fusion
  251.1 76.1 %all-reduce.6.cloned.1.call-done = f32[4,512,128]{2,0,1:T(4,128)} async-done(((f32[4,512,128]{2,0,1:T(4,128)}), f32[4,512,128]{2,0,1:T(4,128)}) %all-reduce.6.cloned.1.call-update) | async-done | bytes 1048592
  327.2 0.9 constant_dynamic-slice_fusion
  328.1 0.7 copy.32
  (5 shorter events, 0.1 us)
Async XLA Ops:
  7.2 3.0 copy-start
  7.2 21.8 %all-gather.5.cloned.1.call-start = ((), (), s32[]{:S(2)}) async-start(), calls=%async_computation.1 | async-start | bytes 1310720 | tf_op jit(solution)/shard_map/all_gather | solution.py:23
  7.9 39.4 %all-gather.3.cloned.1.call-start = ((), (), s32[]{:S(2)}) async-start(), calls=%async_computation | async-start | bytes 1310720 | tf_op jit(solution)/shard_map/all_gather | solution.py:22
  8.7 138.7 %all-reduce.4.cloned.1.call-start = ((), (), s32[]{:S(2)}) async-start(), calls=%async_computation.2 | async-start | bytes 2097152 | tf_op jit(solution)/shard_map/psum | solution.py:39
  62.5 1.3 copy-start.3
  63.9 2.3 copy-start.5
  69.0 258.2 %all-reduce.6.cloned.1.call-start = ((), (), s32[]{:S(2)}) async-start(), calls=%async_computation.3 | async-start | bytes 2097152
  147.4 90.3 %copy-start.2 = (f32[4,512,128]{2,1,0:T(8,128)S(1)}, f32[4,512,128]{2,1,0:T(8,128)}, u32[]{:S(2)}) copy-start(f32[4,512,128]{2,1,0:T(8,128)} %all-reduce.4.cloned.1.call-done) | copy-start | bytes 3145732
  238.8 3.7 %copy-start.4 = (f32[4,8,128,128]{3,2,1,0:T(8,128)S(1)}, f32[4,8,128,128]{3,2,1,0:T(8,128)}, u32[]{:S(2)}) copy-start(f32[4,8,128,128]{3,2,1,0:T(8,128)} %copy-done.3) | copy-start | bytes 6291460
  242.4 3.8 %copy-start.1 = (bf16[4,8,512,128]{3,2,1,0:T(8,128)(2,1)S(1)}, bf16[4,8,512,128]{3,2,1,0:T(8,128)(2,1)}, u32[]{:S(2)}) copy-start(bf16[4,8,512,128]{3,2,1,0:T(8,128)(2,1)} %param.12) | copy-start | bytes 12582916
  246.2 2.9 copy-start.6
Sparse Core Ops, SparseCore 0:
  9.5 19.4 all-gather.4
  30.6 16.6 all-gather.2
  69.1 78.2 all-reduce.3
  249.3 77.8 all-reduce.5
where the time goes:
time: 336 us; the launch traced here: 335 us
  waiting for transfers between devices  178 us (53%)
  other arithmetic  88.8 us (26%)
  matrix products  27 us (8%)
  local copies, waits for them, and re-layouts  26.1 us (8%)
  between operations  14.6 us (4%)
    psum x1, waiting for transfers between devices, body(): summed = lax.psum(partial_sketch, 'inner')  78.1 us
    unnamed x5, waiting for transfers between devices  77.5 us
    another operation x4, other arithmetic, body(): factor = jnp.linalg.cholesky(gram_of(summed))  47.1 us
    another operation x3, other arithmetic, orthonormal(): jax.scipy.linalg.solve_triangular(factor, jnp.swapaxes(sketch_rows, 1, 2)...  39.7 us
    all_gather x1, waiting for transfers between devices, body(): lax.all_gather(left_v, 'cols', axis=0, tiled=True)  15 us
    gather x2, local copies, waits for them, and re-layouts, body(): tile_v = jnp.take(group_v, local_idx, axis=0)  10.6 us
    gather x2, local copies, waits for them, and re-layouts, body(): tile_u = jnp.take(group_u, local_idx, axis=0)  10.5 us
    all_gather x1, waiting for transfers between devices, body(): lax.all_gather(left_u, 'cols', axis=0, tiled=True)  7.72 us
  transfers between devices with their start and end apart: 4, of which 4 were waited for; matrix products, arithmetic and copies ran while one was open for 5% of the time, Pallas kernels for 0%

commit v1 on v0

--- a/solution.py
+++ b/solution.py
@@ -36,7 +36,7 @@
         "osna,osat->ont", tile_u, mixing, preferred_element_type=jnp.float32
     )
     scale_up = math.sqrt(NB)
-    summed = lax.psum(partial_sketch, "inner")
+    summed = jnp.sum(lax.all_gather(partial_sketch, "inner"), axis=0)
     factor = jnp.linalg.cholesky(gram_of(summed))
     ortho = orthonormal(summed, factor)
     row_count = summed.shape[1] // lax.axis_size("inner")

time: 336 us -> 383 us (1.14)
  waiting for transfers between devices: 178 us -> 223 us
  other arithmetic: 88.8 us -> 92.7 us
    all_gather x0 -> x1, waiting for transfers between devices: none -> 124 us  [body(): summed = jnp.sum(lax.all_gather(partial_sketch, 'inner'), axis=0)]
    psum x1 -> x0, waiting for transfers between devices: 78.1 us -> none  [body(): summed = lax.psum(partial_sketch, 'inner')]
    reduce_sum x0 -> x1, other arithmetic: none -> 3.91 us  [body(): summed = jnp.sum(lax.all_gather(partial_sketch, 'inner'), axis=0)]
  transfers between devices with their start and end apart: 4 -> 4, of which waited for: 4 -> 4; matrix products, arithmetic and copies ran while one was open for 5% -> 4% of each run, Pallas kernels for 0% -> 0%
where the time goes in v1:
time: 383 us; the launch traced here: 382 us
  waiting for transfers between devices  223 us (58%)
  other arithmetic  92.7 us (24%)
  local copies, waits for them, and re-layouts  26.2 us (7%)
  matrix products  25.4 us (7%)
  between operations  14.6 us (4%)
    all_gather x1, waiting for transfers between devices, body(): summed = jnp.sum(lax.all_gather(partial_sketch, 'inner'), axis=0)  124 us
    unnamed x5, waiting for transfers between devices  76 us
    another operation x4, other arithmetic, body(): factor = jnp.linalg.cholesky(gram_of(summed))  47.1 us
    another operation x3, other arithmetic, orthonormal(): jax.scipy.linalg.solve_triangular(factor, jnp.swapaxes(sketch_rows, 1, 2)...  39.7 us
    all_gather x1, waiting for transfers between devices, body(): lax.all_gather(left_v, 'cols', axis=0, tiled=True)  15 us
    gather x2, local copies, waits for them, and re-layouts, body(): tile_v = jnp.take(group_v, local_idx, axis=0)  10.6 us
    gather x2, local copies, waits for them, and re-layouts, body(): tile_u = jnp.take(group_u, local_idx, axis=0)  10.5 us
    all_gather x1, waiting for transfers between devices, body(): lax.all_gather(left_u, 'cols', axis=0, tiled=True)  7.72 us
  transfers between devices with their start and end apart: 4, of which 4 were waited for; matrix products, arithmetic and copies ran while one was open for 4% of the time, Pallas kernels for 0%

profile of v1, /device:TPU:0, one launch (start us, length us, event | category | flops | bytes accessed | tf_op | source)
XLA Modules:
  0.0 382.4 jit_solution(5446981819117506402)
XLA Ops:
  7.2 0.0 copy-start
  7.2 0.0 all-gather.7.cloned.1.call-start
  7.2 0.7 all-gather.7.cloned.1.call-update
  7.9 0.0 all-gather.5.cloned.1.call-start
  8.0 0.7 all-gather.5.cloned.1.call-update
  8.7 0.0 all-gather.9.cloned.1.call-start
  8.7 0.7 compare_and_fusion
  9.4 0.1 reshape.42
  9.5 0.7 convert_element_type.12
  10.2 0.0 copy-done
  10.2 3.8 fusion.10
  14.0 15.0 %all-gather.7.cloned.1.call-done = bf16[8,512,128]{2,1,0:T(8,128)(2,1)} async-done(((bf16[2,512,128]{2,1,0:T(8,128)(2,1)}), bf16[8,512,128]{2,1,0:T(8,128)(2,1)}) %all-gather.7.cloned.1.call-update) | async-done | bytes 1048592 | tf_op jit(solution)/shard_map/all_gather | solution.py:23
  29.0 4.3 %gather_fusion.1 = bf16[32,512,128]{2,1,0:T(8,128)(2,1)} fusion(bf16[8,512,128]{2,1,0:T(8,128)(2,1)} %all-gather.7.cloned.1.call-done, s32[1024]{0:T(1024)S(1)} %pad_clamp_fusion), kind=kCustom, calls=%fused_computation.1.clone | custom fusion | bytes 8388736 | tf_op jit(solution)/shard_map/jit(_take)/gather | solution.py:29
  33.3 6.3 %copy.23 = bf16[4,8,512,128]{2,3,1,0:T(8,128)(2,1)} copy(bf16[4,8,512,128]{3,2,1,0:T(8,128)(2,1)} %bitcast.44) | data formatting | bytes 8388608 | tf_op jit(solution)/shard_map/jit(_take)/gather | solution.py:29
  39.6 7.7 %all-gather.5.cloned.1.call-done = bf16[8,512,128]{2,1,0:T(8,128)(2,1)} async-done(((bf16[2,512,128]{2,1,0:T(8,128)(2,1)}), bf16[8,512,128]{2,1,0:T(8,128)(2,1)}) %all-gather.5.cloned.1.call-update) | async-done | bytes 1048592 | tf_op jit(solution)/shard_map/all_gather | solution.py:22
  47.3 4.3 %gather_fusion = bf16[32,512,128]{2,1,0:T(8,128)(2,1)} fusion(bf16[8,512,128]{2,1,0:T(8,128)(2,1)} %all-gather.5.cloned.1.call-done, s32[1024]{0:T(1024)S(1)} %pad_clamp_fusion), kind=kCustom, calls=%fused_computation.clone | custom fusion | bytes 8388736 | tf_op jit(solution)/shard_map/jit(_take)/gather | solution.py:28
  51.6 6.2 %copy.22 = bf16[4,8,512,128]{2,3,1,0:T(8,128)(2,1)} copy(bf16[4,8,512,128]{3,2,1,0:T(8,128)(2,1)} %bitcast.43) | data formatting | bytes 8388608 | tf_op jit(solution)/shard_map/jit(_take)/gather | solution.py:28
  57.8 4.8 %fusion = f32[4,8,128,128]{3,2,1,0:T(8,128)S(1)} fusion(bf16[4,8,512,128]{3,2,1,0:T(8,128)(2,1)} %param.11, bf16[4,8,512,128]{2,3,1,0:T(8,128)(2,1)} %copy.23, pred[4,8]{1,0:T(4,128)(4,1)S(1)} %get-tuple-element.9), kind=kOutput, calls=%fused_computation.2 | convolution fusion | flops 538968064 | bytes 10485792 | tf_op jit(solution)/shard_map/osna,osnb->osab/dot_general | solution.py:30
  62.6 0.0 copy-start.2
  62.6 1.3 copy-done.2
  63.9 0.0 copy-start.4
  63.9 2.3 multiply_convert_fusion.1
  66.2 0.0 copy-done.4
  66.2 2.8 fusion.8
  69.0 0.0 all-gather.9.cloned.1.call-update
  69.1 0.2 all-reduce.3.cloned.1.call-start
  69.3 124.4 %all-gather.9.cloned.1.call-done = f32[32,512,128]{2,1,0:T(8,128)} async-done(((f32[4,512,128]{2,1,0:T(8,128)}), f32[32,512,128]{2,1,0:T(8,128)}) %all-gather.9.cloned.1.call-update) | async-done | bytes 8388624 | tf_op jit(solution)/shard_map/all_gather | solution.py:39
  193.7 3.9 %reduce_sum.9 = f32[4,512,128]{2,1,0:T(8,128)S(1)} reduce(f32[8,4,512,128]{3,2,1,0:T(8,128)} %bitcast.45, f32[]{:T(128)} %constant.64.clone.1), dimensions={0}, to_apply=%region_0.0 | reduce | flops 1835008 | bytes 9437188 | tf_op jit(solution)/shard_map/reduce_sum | solution.py:39
  197.6 1.8 fusion.19
  199.4 0.1 copy.27
  199.6 46.9 %custom-call.8 = f32[4,128,128]{2,1,0:T(8,128)S(1)} custom-call(f32[4,128,128]{2,1,0:T(8,128)S(1)} %fusion.15), custom_call_target="Cholesky" | custom-call | tf_op jit(solution)/shard_map/jit(cholesky)/cholesky | solution.py:40
  246.5 0.1 compare_reduce_fusion
  246.7 0.1 select_bitcast_fusion
  246.8 39.5 %custom-call.9 = f32[4,1,128,128]{2,3,1,0:T(8,128)S(1)} custom-call(f32[4,1,128,128]{3,2,1,0:T(8,128)S(1)} %select_bitcast_fusion), custom_call_target="InvertDiagBlocksLowerTriangular" | custom-call | tf_op jit(solution)/shard_map/jit(_solve_triangular)/vmap()/triangular_solve | solution.py:12
  286.3 1.0 fusion.13
  287.4 0.0 copy-start.3
  287.4 3.6 fusion.3
  291.0 0.0 copy-done.3
  291.0 0.0 copy-start.1
  291.0 3.7 multiply_convert_fusion
  294.8 0.0 copy-done.1
  294.8 0.0 copy-start.5
  294.8 1.5 convolution_bitcast_fusion
  296.3 1.4 copy.31
  297.7 0.0 all-reduce.3.cloned.1.call-update
  297.7 0.0 copy-done.5
  297.7 0.6 dynamic-slice
  299.0 0.7 dynamic-slice_multiply_fusion
  299.7 74.6 %all-reduce.3.cloned.1.call-done = f32[4,512,128]{2,0,1:T(4,128)} async-done(((f32[4,512,128]{2,0,1:T(4,128)}), f32[4,512,128]{2,0,1:T(4,128)}) %all-reduce.3.cloned.1.call-update) | async-done | bytes 1048592
  374.3 0.9 constant_dynamic-slice_fusion
  375.2 0.7 copy.32
  (5 shorter events, 0.1 us)
Async XLA Ops:
  7.2 3.0 copy-start
  7.2 21.8 %all-gather.7.cloned.1.call-start = ((), (), s32[]{:S(2)}) async-start(), calls=%async_computation.1 | async-start | bytes 1310720 | tf_op jit(solution)/shard_map/all_gather | solution.py:23
  7.9 39.4 %all-gather.5.cloned.1.call-start = ((), (), s32[]{:S(2)}) async-start(), calls=%async_computation | async-start | bytes 1310720 | tf_op jit(solution)/shard_map/all_gather | solution.py:22
  8.7 185.0 %all-gather.9.cloned.1.call-start = ((), (), s32[]{:S(2)}) async-start(), calls=%async_computation.2 | async-start | bytes 9437184 | tf_op jit(solution)/shard_map/all_gather | solution.py:39
  62.6 1.3 copy-start.2
  63.9 2.3 copy-start.4
  69.1 305.2 %all-reduce.3.cloned.1.call-start = ((), (), s32[]{:S(2)}) async-start(), calls=%async_computation.3 | async-start | bytes 2097152
  287.4 3.7 copy-start.3
  291.0 3.8 copy-start.1
  294.8 2.9 copy-start.5
Sparse Core Ops, SparseCore 0:
  9.5 19.4 all-gather.6
  30.6 16.6 all-gather.4
  69.2 124.4 all-gather.8
  297.8 76.3 all-reduce.2
